TPU v7x, 32 devices: a whole 2x2x4 slice. The times are simulated.
32 devices in a mesh: group: 2 (over x), blk: 8 (over z, y), ulysses: 2 (over core).
Axes of the slice: x: 2, y: 2, z: 4, core: 2. Of those that a mesh axis runs over, the one named last changes fastest.
Arguments:
- query_int: bfloat16 [4096, 8192], P(('group', 'blk', 'ulysses')), parts along dimension 0, may hold values from -127 to 127, as said below
- key_int: bfloat16 [4096, 1024], P(('group', 'blk', 'ulysses')), parts along dimension 0, may hold values from -127 to 127, as said below
- values: bfloat16 [4096, 1024], P(('group', 'blk', 'ulysses')), parts along dimension 0, may hold values from -6 to 6
- query_scale: bfloat16 [32, 64], P(('group', 'blk')), parts along dimension 0, may hold values from 0.001 to 0.02
- key_scale: bfloat16 [32, 8], P('group'), parts along dimension 0, may hold values from 0.002 to 0.04
- verticals: int32 [16, 8], P('group'), parts along dimension 0, may hold values from 0 to 15, as said below
- slashes: int32 [16, 8], P('group'), parts along dimension 0, may hold values from 0 to 8, as said below
Outputs:
- attention: bfloat16 [4096, 8192], P(('group', 'blk', 'ulysses')), parts along dimension 0
There are 2 independent parts, one for each index of `group`. A program takes and returns all parts, laid end to end along the dimension named above; each array names one. Nothing has to cross between parts.
Inputs may be any that keep to these rules, and one draw needn't show every extreme that they name: `query_int`: integer values. `key_int`: integer values. `verticals`: each row holds 8 distinct key blocks, block 0 among them. `slashes`: each row holds 8 distinct offsets, 0 among them.
All inputs are finite; a program needn't handle non-finite values.
Results may differ from a plain program's by a relative error of at most 0.0019.
Values may be sent and summed in bfloat16 or wider, within the bound.
A program may use at most 128 MiB of HBM per device.

v0:
```python
import jax
import jax.numpy as jnp
from jax import lax
from jax.sharding import PartitionSpec as P

DH = 128
BLOCK = 128
FLOOR_SCORE = -1e30


def block_table(verticals, slashes, first_block, block_count):
    blocks = first_block + jnp.arange(block_count, dtype=jnp.int32)
    slash_keys = blocks[:, None, None] - slashes[None, :, :]
    slash_live = slash_keys >= 0
    vert_keys = jnp.broadcast_to(verticals[None, :, :], (block_count,) + verticals.shape)
    clashes = jnp.any(
        (vert_keys[:, :, :, None] == slash_keys[:, :, None, :]) & slash_live[:, :, None, :], axis=3
    )
    vert_live = (vert_keys <= blocks[:, None, None]) & jnp.logical_not(clashes)
    return (
        jnp.concatenate([vert_keys, slash_keys], axis=2),
        jnp.concatenate([vert_live, slash_live], axis=2),
        blocks,
    )


def gather_blocks(buffer, positions, groups):
    shaped = buffer.reshape(buffer.shape[0] // BLOCK, BLOCK, groups, DH)
    heads_at = jnp.arange(groups, dtype=jnp.int32)[None, :, None]
    return shaped[positions, :, heads_at, :]


def attend_group(pieces):
    query_block, query_scales, key_blocks, value_blocks, key_scales, live_slots, diagonal = pieces
    dots = jnp.einsum("tpd,nsd->ptns", query_block, key_blocks, preferred_element_type=jnp.float32)
    scores = dots * query_scales[:, None, None, None] * key_scales[None, None, :, None]
    width = query_block.shape[0]
    causal = jnp.arange(width)[None, :] <= jnp.arange(width)[:, None]
    allowed = live_slots[None, None, :, None] & (
        jnp.logical_not(diagonal)[None, None, :, None] | causal[None, :, None, :]
    )
    masked = jnp.where(allowed, scores, FLOOR_SCORE)
    largest = jnp.max(masked, axis=(2, 3), keepdims=True)
    weights = jnp.where(allowed, jnp.exp(masked - largest), 0.0)
    totals = jnp.sum(weights, axis=(2, 3))
    numer = jnp.einsum(
        "ptns,nsd->tpd",
        weights.astype(jnp.bfloat16),
        value_blocks,
        preferred_element_type=jnp.float32,
    )
    return (numer / jnp.transpose(totals, (1, 0))[:, :, None]).astype(jnp.bfloat16)


def attend_block(pieces):
    query_block, query_scales, key_blocks, value_blocks, key_scales, live_slots, diagonal = pieces
    by_group = lax.map(
        attend_group,
        (
            jnp.transpose(query_block, (1, 0, 2, 3)),
            query_scales,
            key_blocks,
            value_blocks,
            key_scales,
            live_slots,
            diagonal,
        ),
    )
    return jnp.transpose(by_group, (1, 0, 2, 3))


def local(query_int, key_int, values, query_scale, key_scale, verticals, slashes):
    query_here, key_here, value_here = (
        lax.all_to_all(query_int, "ulysses", split_axis=1, concat_axis=0, tiled=True),
        lax.all_to_all(key_int, "ulysses", split_axis=1, concat_axis=0, tiled=True),
        lax.all_to_all(values, "ulysses", split_axis=1, concat_axis=0, tiled=True),
    )
    half_index = lax.axis_index("ulysses")
    span_index = lax.axis_index("blk")
    span_rows = query_here.shape[0]
    block_count = span_rows // BLOCK
    heads_here = query_here.shape[1] // DH
    groups_here = key_here.shape[1] // DH
    per_group = heads_here // groups_here
    first_block = span_index * block_count
    group_ids = half_index * groups_here + jnp.arange(groups_here, dtype=jnp.int32)
    query_scales = lax.dynamic_slice_in_dim(query_scale, half_index * heads_here, heads_here, 1)
    query_scales = query_scales.astype(jnp.float32).reshape(block_count, groups_here, per_group)
    vert_here = lax.dynamic_slice_in_dim(verticals, half_index * groups_here, groups_here, 0)
    slash_here = lax.dynamic_slice_in_dim(slashes, half_index * groups_here, groups_here, 0)
    block_keys, live_slots, blocks = block_table(vert_here, slash_here, first_block, block_count)
    total_blocks = key_scale.shape[0]
    clipped = jnp.clip(block_keys, 0, total_blocks - 1)
    key_scales = key_scale[clipped, group_ids[None, :, None]].astype(jnp.float32)
    key_all, value_all = (
        lax.all_gather(key_here, "blk", axis=0, tiled=True),
        lax.all_gather(value_here, "blk", axis=0, tiled=True),
    )
    key_blocks = gather_blocks(key_all, clipped, groups_here)
    value_blocks = gather_blocks(value_all, clipped, groups_here)
    diagonal = block_keys == blocks[:, None, None]
    query_blocks = query_here.reshape(block_count, BLOCK, groups_here, per_group, DH)
    outputs = lax.map(
        attend_block,
        (query_blocks, query_scales, key_blocks, value_blocks, key_scales, live_slots, diagonal),
    )
    merged = outputs.reshape(span_rows, heads_here * DH)
    return lax.all_to_all(merged, "ulysses", split_axis=0, concat_axis=1, tiled=True)


def solution(mesh):
    in_specs = (
        P(("group", "blk", "ulysses"), None),
        P(("group", "blk", "ulysses"), None),
        P(("group", "blk", "ulysses"), None),
        P(("group", "blk"), None),
        P("group", None),
        P("group", None),
        P("group", None),
    )
    out_specs = P(("group", "blk", "ulysses"), None)
    return jax.shard_map(local, mesh=mesh, in_specs=in_specs, out_specs=out_specs, check_vma=False)
```

profile of v0, /device:TPU:0, one launch (start us, length us, event | category | flops | bytes accessed | tf_op | source)
XLA Modules:
  0.0 241.5 jit_solution(8448017913891180040)
XLA Ops:
  6.5 1.3 copy.58
  7.8 3.9 %all_to_all.73 = bf16[128,2,512]{0,2,1:T(8,128)(2,1)S(1)} all-to-all(bf16[128,2,512]{0,2,1:T(8,128)(2,1)S(1)} %bitcast.156), channel_id=1, replica_groups=mesh['group'=2,'blk'=8,'ulysses'=2] {'ulysses'}, dimensions={1} | all-to-all | bytes 524288 | tf_op jit(solution)/shard_map/all_to_all | solution.py:75
  11.8 0.8 copy.59
  12.7 1.1 copy.62
  13.8 3.9 %all_to_all.74 = bf16[128,2,512]{0,2,1:T(8,128)(2,1)S(1)} all-to-all(bf16[128,2,512]{0,2,1:T(8,128)(2,1)S(1)} %bitcast.157), channel_id=1, replica_groups=mesh['group'=2,'blk'=8,'ulysses'=2] {'ulysses'}, dimensions={1} | all-to-all | bytes 524288 | tf_op jit(solution)/shard_map/all_to_all | solution.py:76
  17.7 0.9 copy.63
  18.7 2.4 %copy.57 = bf16[128,8192]{0,1:T(8,128)(2,1)} copy(bf16[128,8192]{1,0:T(8,128)(2,1)S(1)} %copy-done.1) | data formatting | bytes 4194304 | tf_op args[0]
  21.1 5.0 %all-to-all-start = ((bf16[128,2,4096]{0,2,1:T(8,128)(2,1)}), bf16[128,2,4096]{0,2,1:T(8,128)(2,1)}, u32[]{:S(2)}, u32[]{:S(2)}) async-start(bf16[128,2,4096]{0,2,1:T(8,128)(2,1)} %bitcast.27), calls=%async_computation | async-start | bytes 4194304 | tf_op jit(solution)/shard_map/all_to_all | solution.py:74
  26.6 1.5 gather_fusion.2
  28.4 0.3 and_reduce_fusion
  28.9 35.7 %all-gather.3.cloned.1.call-done = bf16[2048,512]{1,0:T(8,128)(2,1)} async-done(((bf16[256,512]{1,0:T(8,128)(2,1)}), bf16[2048,512]{1,0:T(8,128)(2,1)}) %all-gather.3.cloned.1.call-update) | async-done | bytes 2097168 | tf_op jit(solution)/shard_map/all_gather | solution.py:96
  64.6 4.0 %reshape.141 = bf16[16,128,4,128]{3,2,1,0:T(4,128)(2,1)} reshape(bf16[2048,512]{1,0:T(8,128)(2,1)} %all-gather.3.cloned.1.call-done) | data formatting | bytes 4194304 | tf_op jit(solution)/shard_map/reshape | solution.py:28
  68.6 2.1 copy.61
  70.7 43.7 %all-gather.5.cloned.1.call-done = bf16[2048,512]{1,0:T(8,128)(2,1)} async-done(((bf16[256,512]{1,0:T(8,128)(2,1)}), bf16[2048,512]{1,0:T(8,128)(2,1)}) %all-gather.5.cloned.1.call-update) | async-done | bytes 2097168 | tf_op jit(solution)/shard_map/all_gather | solution.py:97
  114.4 4.0 %reshape.142 = bf16[16,128,4,128]{3,2,1,0:T(4,128)(2,1)} reshape(bf16[2048,512]{1,0:T(8,128)(2,1)} %all-gather.5.cloned.1.call-done) | data formatting | bytes 4194304 | tf_op jit(solution)/shard_map/reshape | solution.py:28
  118.3 3.5 %copy.65 = bf16[16,128,4,128]{3,1,2,0:T(8,128)(2,1)} copy(bf16[16,128,4,128]{3,2,1,0:T(4,128)(2,1)} %reshape.142) | data formatting | bytes 4194304 | tf_op jit(solution)/shard_map/reshape | solution.py:28
  121.8 3.1 %gather_fusion = bf16[128,128,128]{2,1,0:T(8,128)(2,1)} fusion(bf16[16,128,4,128]{3,1,2,0:T(8,128)(2,1)S(1)} %copy.61, s32[128]{0:T(128)S(1)} %reshape.118), kind=kCustom, calls=%fused_computation | custom fusion | bytes 8389632 | tf_op jit(solution)/shard_map/gather | solution.py:30
  124.9 4.7 %gather_fusion.1 = bf16[128,128,128]{2,1,0:T(8,128)(2,1)} fusion(bf16[16,128,4,128]{3,1,2,0:T(8,128)(2,1)} %copy.65, s32[128]{0:T(128)S(1)} %reshape.118), kind=kCustom, calls=%fused_computation.1 | custom fusion | bytes 8389632 | tf_op jit(solution)/shard_map/gather | solution.py:30
  129.6 89.9 %while.21 = (s32[]{:T(128)}, bf16[2,128,4,8,128]{1,4,3,2,0:T(8,128)(2,1)}, bf16[2,128,4,8,128]{1,4,3,2,0:T(8,128)(2,1)}, f32[2,4,8]{2,1,0:T(4,128)S(1)}, bf16[2,...) while((s32[]{:T(128)}, ...), condition=%wide.region_6.7_spmd, body=%wide.region_1.6_spmd.sunk | while | flops 1108097024 | bytes 46721236 | solution.py:103
  129.6 1.7 constant_dynamic-slice_fusion.13
  131.3 2.6 %copy.84 = bf16[1,4,16,128,128]{3,4,2,1,0:T(8,128)(2,1)} copy(bf16[1,4,16,128,128]{4,3,2,1,0:T(8,128)(2,1)S(1)} %constant_dynamic-slice_fusion.13) | data formatting | bytes 4194304 | tf_op jit(solution)/shard_map/while/body/jit(dynamic_index_in_dim)/dynamic_slice | solution.py:103
  133.9 1.3 constant_dynamic-slice_fusion.14
  135.2 1.4 copy.85
  136.6 1.7 dynamic-slice_bitcast_fusion.6
  138.3 35.1 %while.22 = (s32[]{:T(128)}, bf16[4,128,8,128]{1,3,2,0:T(8,128)(2,1)S(1)}, bf16[4,16,128,128]{2,3,1,0:T(8,128)(2,1)}, pred[4,16]{1,0:T(4,128)(4,1)S(1)}, pred[4,...) while((s32[]{:T(128)}, ...), condition=%wide.region_5.5_spmd, body=%wide.region_2.4_spmd.sunk | while | flops 1108097024 | bytes 27845104 | solution.py:57
  138.4 0.2 or_and_fusion.2
  138.7 2.4 fusion.58
  141.1 2.4 fusion.59
  143.5 3.6 %fusion.60 = bf16[4,128,8,128]{1,3,2,0:T(8,128)(2,1)S(1)} fusion(bf16[4,128,8,128]{1,3,2,0:T(8,128)(2,1)S(1)} %get-tuple-element.347, s32[]{:T(128)} %get-tuple-element.346, f32[16,128,128,8]{2,1,3,0:T(8,128)S(1)} %get-tuple-element.334, f32[8,128]{1,0:T(8,128)S(1)} %get-tuple-element.335, f32[16]{0:T(128)S(1)} %fusion.55, f32[8]{0:T(128)S(1)} %fusion.56, ...), kind=kOutput, calls=%fused_computation.14.clone.1 | convolution fusion | flops 549715968 | bytes 9447424 | tf_op jit(solution)/shard_map/while/body/eval_jaxpr/while/body/eval_jaxpr/ptns,nsd->tpd/dot_general | solution.py:46
  147.2 0.2 or_and_fusion.2
  147.5 2.4 fusion.58
  149.9 2.4 fusion.59
  152.3 3.6 %fusion.60 = bf16[4,128,8,128]{1,3,2,0:T(8,128)(2,1)S(1)} fusion(bf16[4,128,8,128]{1,3,2,0:T(8,128)(2,1)S(1)} %get-tuple-element.347, s32[]{:T(128)} %get-tuple-element.346, f32[16,128,128,8]{2,1,3,0:T(8,128)S(1)} %get-tuple-element.334, f32[8,128]{1,0:T(8,128)S(1)} %get-tuple-element.335, f32[16]{0:T(128)S(1)} %fusion.55, f32[8]{0:T(128)S(1)} %fusion.56, ...), kind=kOutput, calls=%fused_computation.14.clone.1 | convolution fusion | flops 549715968 | bytes 9447424 | tf_op jit(solution)/shard_map/while/body/eval_jaxpr/while/body/eval_jaxpr/ptns,nsd->tpd/dot_general | solution.py:46
  156.2 2.4 fusion.58
  158.6 2.4 fusion.59
  161.1 3.6 %fusion.60 = bf16[4,128,8,128]{1,3,2,0:T(8,128)(2,1)S(1)} fusion(bf16[4,128,8,128]{1,3,2,0:T(8,128)(2,1)S(1)} %get-tuple-element.347, s32[]{:T(128)} %get-tuple-element.346, f32[16,128,128,8]{2,1,3,0:T(8,128)S(1)} %get-tuple-element.334, f32[8,128]{1,0:T(8,128)S(1)} %get-tuple-element.335, f32[16]{0:T(128)S(1)} %fusion.55, f32[8]{0:T(128)S(1)} %fusion.56, ...), kind=kOutput, calls=%fused_computation.14.clone.1 | convolution fusion | flops 549715968 | bytes 9447424 | tf_op jit(solution)/shard_map/while/body/eval_jaxpr/while/body/eval_jaxpr/ptns,nsd->tpd/dot_general | solution.py:46
  164.7 0.2 or_and_fusion.2
  165.0 2.4 fusion.58
  167.4 2.4 fusion.59
  169.8 3.6 %fusion.60 = bf16[4,128,8,128]{1,3,2,0:T(8,128)(2,1)S(1)} fusion(bf16[4,128,8,128]{1,3,2,0:T(8,128)(2,1)S(1)} %get-tuple-element.347, s32[]{:T(128)} %get-tuple-element.346, f32[16,128,128,8]{2,1,3,0:T(8,128)S(1)} %get-tuple-element.334, f32[8,128]{1,0:T(8,128)S(1)} %get-tuple-element.335, f32[16]{0:T(128)S(1)} %fusion.55, f32[8]{0:T(128)S(1)} %fusion.56, ...), kind=kOutput, calls=%fused_computation.14.clone.1 | convolution fusion | flops 549715968 | bytes 9447424 | tf_op jit(solution)/shard_map/while/body/eval_jaxpr/while/body/eval_jaxpr/ptns,nsd->tpd/dot_general | solution.py:46
  173.5 1.0 bitcast_dynamic-update-slice_fusion.2
  174.5 1.7 constant_dynamic-slice_fusion.13
  176.2 2.6 %copy.84 = bf16[1,4,16,128,128]{3,4,2,1,0:T(8,128)(2,1)} copy(bf16[1,4,16,128,128]{4,3,2,1,0:T(8,128)(2,1)S(1)} %constant_dynamic-slice_fusion.13) | data formatting | bytes 4194304 | tf_op jit(solution)/shard_map/while/body/jit(dynamic_index_in_dim)/dynamic_slice | solution.py:103
  178.8 1.3 constant_dynamic-slice_fusion.14
  180.1 1.4 copy.85
  181.5 1.7 dynamic-slice_bitcast_fusion.6
  183.3 35.1 %while.22 = (s32[]{:T(128)}, bf16[4,128,8,128]{1,3,2,0:T(8,128)(2,1)S(1)}, bf16[4,16,128,128]{2,3,1,0:T(8,128)(2,1)}, pred[4,16]{1,0:T(4,128)(4,1)S(1)}, pred[4,...) while((s32[]{:T(128)}, ...), condition=%wide.region_5.5_spmd, body=%wide.region_2.4_spmd.sunk | while | flops 1108097024 | bytes 27845104 | solution.py:57
  183.6 2.4 fusion.58
  186.0 2.4 fusion.59
  188.4 3.6 %fusion.60 = bf16[4,128,8,128]{1,3,2,0:T(8,128)(2,1)S(1)} fusion(bf16[4,128,8,128]{1,3,2,0:T(8,128)(2,1)S(1)} %get-tuple-element.347, s32[]{:T(128)} %get-tuple-element.346, f32[16,128,128,8]{2,1,3,0:T(8,128)S(1)} %get-tuple-element.334, f32[8,128]{1,0:T(8,128)S(1)} %get-tuple-element.335, f32[16]{0:T(128)S(1)} %fusion.55, f32[8]{0:T(128)S(1)} %fusion.56, ...), kind=kOutput, calls=%fused_computation.14.clone.1 | convolution fusion | flops 549715968 | bytes 9447424 | tf_op jit(solution)/shard_map/while/body/eval_jaxpr/while/body/eval_jaxpr/ptns,nsd->tpd/dot_general | solution.py:46
  192.4 2.4 fusion.58
  194.8 2.4 fusion.59
  197.2 3.6 %fusion.60 = bf16[4,128,8,128]{1,3,2,0:T(8,128)(2,1)S(1)} fusion(bf16[4,128,8,128]{1,3,2,0:T(8,128)(2,1)S(1)} %get-tuple-element.347, s32[]{:T(128)} %get-tuple-element.346, f32[16,128,128,8]{2,1,3,0:T(8,128)S(1)} %get-tuple-element.334, f32[8,128]{1,0:T(8,128)S(1)} %get-tuple-element.335, f32[16]{0:T(128)S(1)} %fusion.55, f32[8]{0:T(128)S(1)} %fusion.56, ...), kind=kOutput, calls=%fused_computation.14.clone.1 | convolution fusion | flops 549715968 | bytes 9447424 | tf_op jit(solution)/shard_map/while/body/eval_jaxpr/while/body/eval_jaxpr/ptns,nsd->tpd/dot_general | solution.py:46
  201.2 2.4 fusion.58
  203.6 2.4 fusion.59
  206.0 3.6 %fusion.60 = bf16[4,128,8,128]{1,3,2,0:T(8,128)(2,1)S(1)} fusion(bf16[4,128,8,128]{1,3,2,0:T(8,128)(2,1)S(1)} %get-tuple-element.347, s32[]{:T(128)} %get-tuple-element.346, f32[16,128,128,8]{2,1,3,0:T(8,128)S(1)} %get-tuple-element.334, f32[8,128]{1,0:T(8,128)S(1)} %get-tuple-element.335, f32[16]{0:T(128)S(1)} %fusion.55, f32[8]{0:T(128)S(1)} %fusion.56, ...), kind=kOutput, calls=%fused_computation.14.clone.1 | convolution fusion | flops 549715968 | bytes 9447424 | tf_op jit(solution)/shard_map/while/body/eval_jaxpr/while/body/eval_jaxpr/ptns,nsd->tpd/dot_general | solution.py:46
  209.9 2.4 fusion.58
  212.3 2.4 fusion.59
  214.8 3.6 %fusion.60 = bf16[4,128,8,128]{1,3,2,0:T(8,128)(2,1)S(1)} fusion(bf16[4,128,8,128]{1,3,2,0:T(8,128)(2,1)S(1)} %get-tuple-element.347, s32[]{:T(128)} %get-tuple-element.346, f32[16,128,128,8]{2,1,3,0:T(8,128)S(1)} %get-tuple-element.334, f32[8,128]{1,0:T(8,128)S(1)} %get-tuple-element.335, f32[16]{0:T(128)S(1)} %fusion.55, f32[8]{0:T(128)S(1)} %fusion.56, ...), kind=kOutput, calls=%fused_computation.14.clone.1 | convolution fusion | flops 549715968 | bytes 9447424 | tf_op jit(solution)/shard_map/while/body/eval_jaxpr/while/body/eval_jaxpr/ptns,nsd->tpd/dot_general | solution.py:46
  218.4 1.0 bitcast_dynamic-update-slice_fusion.2
  219.4 2.9 %copy.79 = bf16[2,128,4096]{2,1,0:T(8,128)(2,1)S(1)} copy(bf16[2,128,4096]{1,2,0:T(8,128)(2,1)} %bitcast.151) | data formatting | bytes 4194304 | tf_op jit(solution)/shard_map/all_to_all | solution.py:108
  222.4 6.3 %all_to_all.75 = bf16[2,128,4096]{2,1,0:T(8,128)(2,1)} all-to-all(bf16[2,128,4096]{2,1,0:T(8,128)(2,1)S(1)} %copy.79), channel_id=1, replica_groups=mesh['group'=2,'blk'=8,'ulysses'=2] {'ulysses'}, dimensions={0} | all-to-all | bytes 4194304 | tf_op jit(solution)/shard_map/all_to_all | solution.py:108
  228.7 3.1 %copy.69 = bf16[2,128,4096]{1,2,0:T(8,128)(2,1)S(1)} copy(bf16[2,128,4096]{2,1,0:T(8,128)(2,1)} %all_to_all.75) | data formatting | bytes 4194304 | tf_op jit(solution)/shard_map/all_to_all | solution.py:108
  231.8 2.9 %copy.70 = bf16[128,8192]{1,0:T(8,128)(2,1)} copy(bf16[128,8192]{0,1:T(8,128)(2,1)S(1)} %bitcast.149) | data formatting | bytes 4194304 | tf_op jit(solution)/shard_map/all_to_all | solution.py:108
  (77 shorter events, 2.6 us)
Async XLA Ops:
  6.5 20.0 %copy-start = (bf16[16,8]{0,1:T(8,128)(2,1)S(1)}, bf16[16,8]{0,1:T(8,128)(2,1)}, u32[]{:S(2)}) copy-start(bf16[16,8]{0,1:T(8,128)(2,1)} %param.15) | copy-start | bytes 772
  6.5 12.1 %copy-start.1 = (bf16[128,8192]{1,0:T(8,128)(2,1)S(1)}, bf16[128,8192]{1,0:T(8,128)(2,1)}, u32[]{:S(2)}) copy-start(bf16[128,8192]{1,0:T(8,128)(2,1)} %param.11) | copy-start | bytes 6291460
  6.5 58.1 %all-gather.3.cloned.1.call-start = ((), (), s32[]{:S(2)}) async-start(), calls=%async_computation.4 | async-start | bytes 2359296 | tf_op jit(solution)/shard_map/all_gather | solution.py:96
  12.6 101.7 %all-gather.5.cloned.1.call-start = ((), (), s32[]{:S(2)}) async-start(), calls=%async_computation.5 | async-start | bytes 2359296 | tf_op jit(solution)/shard_map/all_gather | solution.py:97
  18.6 7.6 %copy-start.2 = (s32[8,8]{1,0:T(8,128)S(1)}, s32[8,8]{1,0:T(8,128)}, u32[]{:S(2)}) copy-start(s32[8,8]{1,0:T(8,128)} %param.17) | copy-start | bytes 772
  18.7 7.6 %copy-start.3 = (s32[8,8]{1,0:T(8,128)S(1)}, s32[8,8]{1,0:T(8,128)}, u32[]{:S(2)}) copy-start(s32[8,8]{1,0:T(8,128)} %param.16) | copy-start | bytes 772
  21.1 7.1 %copy-start.4 = (bf16[2,64]{1,0:T(2,128)(2,1)S(1)}, bf16[2,64]{1,0:T(2,128)(2,1)}, u32[]{:S(2)}) copy-start(bf16[2,64]{1,0:T(2,128)(2,1)} %param.14) | copy-start | bytes 772
  21.1 108.5 %all-to-all-start = ((bf16[128,2,4096]{0,2,1:T(8,128)(2,1)}), bf16[128,2,4096]{0,2,1:T(8,128)(2,1)}, u32[]{:S(2)}, u32[]{:S(2)}) async-start(bf16[128,2,4096]{0,2,1:T(8,128)(2,1)} %bitcast.27), calls=%async_computation | async-start | bytes 4194304 | tf_op jit(solution)/shard_map/all_to_all | solution.py:74
Sparse Core Ops, SparseCore 0:
  12.8 51.8 all-gather.2
  66.7 47.5 all-gather.4
where the time goes:
time: 243 us; the launch traced here: 242 us
  waiting for transfers between devices  79.3 us (33%)
  local copies, waits for them, and re-layouts  58.4 us (24%)
  matrix products  48.1 us (20%)
  other arithmetic  22.2 us (9%)
  blocking collectives  14.2 us (6%)
  between operations  13.6 us (6%)
  starting transfers between devices  5.08 us (2%)
    all_gather x1, waiting for transfers between devices, local(): lax.all_gather(value_here, 'blk', axis=0, tiled=True)  43.7 us
    all_gather x1, waiting for transfers between devices, local(): lax.all_gather(key_here, 'blk', axis=0, tiled=True)  35.7 us
    dot_general x8, matrix products, attend_group(): jnp.einsum('ptns,nsd->tpd', weights.astype(jnp.bfloat16), value_blocks, p...  28.8 us
    reduce_sum x8, other arithmetic, attend_group(): totals = jnp.sum(weights, axis=(2, 3))  19.3 us
    dot_general x8, matrix products, attend_group(): jnp.einsum('tpd,nsd->ptns', query_block, key_blocks, preferred_element_ty...  19.2 us
    dynamic_slice x8, local copies, waits for them, and re-layouts, local(): lax.map(attend_block, (query_blocks, query_scales, key_blocks, value_bloc...  14 us
    reshape x4, local copies, waits for them, and re-layouts, gather_blocks(): shaped = buffer.reshape(buffer.shape[0] // BLOCK, BLOCK, groups, DH)  13.5 us
    all_to_all x3, local copies, waits for them, and re-layouts, local(): lax.all_to_all(merged, 'ulysses', split_axis=0, concat_axis=1, tiled=True)  8.94 us
  transfers between devices with their start and end apart: 3, of which 2 were waited for; matrix products, arithmetic and copies ran while one was open for 12% of the time, Pallas kernels for 0%

commit v1 on v0

--- a/solution.py
+++ b/solution.py
@@ -6,6 +6,28 @@
 DH = 128
 BLOCK = 128
 FLOOR_SCORE = -1e30
+
+
+def laid_out(pieces, dim):
+    pieces = jnp.moveaxis(pieces, 0, dim)
+    shape = pieces.shape
+    return pieces.reshape(*shape[:dim], shape[dim] * shape[dim + 1], *shape[dim + 2 :])
+
+
+def gather_around(x, axis, dim):
+    size = lax.axis_size(axis)
+    pairs = [(i, (i + 1) % size) for i in range(size)]
+    back = [(b, a) for a, b in pairs]
+    lower, upper = ([], [])
+    for step in range(size - 1):
+        if step % 2 == 0:
+            lower.append(lax.ppermute(lower[-1] if lower else x, axis, pairs))
+        else:
+            upper.append(lax.ppermute(upper[-1] if upper else x, axis, back))
+    tiles = jnp.stack([*lower[::-1], x, *upper])
+    shift = lax.axis_index(axis) - len(lower)
+    tiles = tiles[(jnp.arange(size) - shift) % size]
+    return laid_out(tiles, dim)
 
 
 def block_table(verticals, slashes, first_block, block_count):
@@ -93,7 +115,7 @@
     clipped = jnp.clip(block_keys, 0, total_blocks - 1)
     key_scales = key_scale[clipped, group_ids[None, :, None]].astype(jnp.float32)
     key_all, value_all = (
-        lax.all_gather(key_here, "blk", axis=0, tiled=True),
+        gather_around(key_here, "blk", 0),
         lax.all_gather(value_here, "blk", axis=0, tiled=True),
     )
     key_blocks = gather_blocks(key_all, clipped, groups_here)

time: 243 us -> 221 us (0.909)
  waiting for transfers between devices: 79.3 us -> 36.3 us
  starting transfers between devices: 5.08 us -> 23.5 us
  local copies, waits for them, and re-layouts: 58.4 us -> 61.1 us
    all_gather x1, waiting for transfers between devices: 43.7 us -> 0.01 us  [local(): lax.all_gather(value_here, 'blk', axis=0, tiled=True)]
    ppermute x0 -> x7, waiting for transfers between devices: none -> 36.3 us  [the longest x4 36.3 us: gather_around(): lower.append(lax.ppermute(lower[-1] if lower else x, axis, pairs))]
    all_gather x1 -> x0, waiting for transfers between devices: 35.7 us -> none  [local(): lax.all_gather(key_here, 'blk', axis=0, tiled=True)]
    ppermute x0 -> x7, starting transfers between devices: none -> 18.5 us  [the longest x3 12.9 us: gather_around(): upper.append(lax.ppermute(upper[-1] if upper else x, axis, back))]
    reshape x4 -> x2, local copies, waits for them, and re-layouts: 13.5 us -> 6.17 us  [gather_blocks(): shaped = buffer.reshape(buffer.shape[0] // BLOCK, BLOCK, groups, DH)]
    unnamed x13 -> x20, local copies, waits for them, and re-layouts: 4.85 us -> 9.93 us
    another operation x0 -> x3, local copies, waits for them, and re-layouts: none -> 5.02 us  [the longest x2 4.26 us: gather_blocks(): shaped = buffer.reshape(buffer.shape[0] // BLOCK, BLOCK, groups, DH)]
  transfers between devices with their start and end apart: 3 -> 9, of which waited for: 2 -> 3; matrix products, arithmetic and copies ran while one was open for 12% -> 15% of each run, Pallas kernels for 0% -> 0%
where the time goes in v1:
time: 221 us; the launch traced here: 220 us
  local copies, waits for them, and re-layouts  61.1 us (28%)
  matrix products  48.1 us (22%)
  waiting for transfers between devices  36.3 us (16%)
  starting transfers between devices  23.5 us (11%)
  other arithmetic  22.2 us (10%)
  blocking collectives  14.2 us (6%)
  between operations  13.6 us (6%)
    ppermute x4, waiting for transfers between devices, gather_around(): lower.append(lax.ppermute(lower[-1] if lower else x, axis, pairs))  36.3 us
    dot_general x8, matrix products, attend_group(): jnp.einsum('ptns,nsd->tpd', weights.astype(jnp.bfloat16), value_blocks, p...  28.8 us
    reduce_sum x8, other arithmetic, attend_group(): totals = jnp.sum(weights, axis=(2, 3))  19.3 us
    dot_general x8, matrix products, attend_group(): jnp.einsum('tpd,nsd->ptns', query_block, key_blocks, preferred_element_ty...  19.2 us
    dynamic_slice x8, local copies, waits for them, and re-layouts, local(): lax.map(attend_block, (query_blocks, query_scales, key_blocks, value_bloc...  13.9 us
    ppermute x3, starting transfers between devices, gather_around(): upper.append(lax.ppermute(upper[-1] if upper else x, axis, back))  12.9 us
    unnamed x20, local copies, waits for them, and re-layouts  9.93 us
    all_to_all x3, local copies, waits for them, and re-layouts, local(): lax.all_to_all(merged, 'ulysses', split_axis=0, concat_axis=1, tiled=True)  8.94 us
  transfers between devices with their start and end apart: 9, of which 3 were waited for; matrix products, arithmetic and copies ran while one was open for 15% of the time, Pallas kernels for 0%

profile of v1, /device:TPU:0, one launch (start us, length us, event | category | flops | bytes accessed | tf_op | source)
XLA Modules:
  0.0 219.7 jit_solution(13252557533301178345)
XLA Ops:
  6.5 1.3 copy.61
  7.8 3.9 %all_to_all.73 = bf16[128,2,512]{0,2,1:T(8,128)(2,1)S(1)} all-to-all(bf16[128,2,512]{0,2,1:T(8,128)(2,1)S(1)} %bitcast.177), channel_id=1, replica_groups=mesh['group'=2,'blk'=8,'ulysses'=2] {'ulysses'}, dimensions={1} | all-to-all | bytes 524288 | tf_op jit(solution)/shard_map/all_to_all | solution.py:97
  11.9 3.0 %collective-permute-start = (bf16[256,512]{1,0:T(8,128)(2,1)S(1)}, bf16[256,512]{1,0:T(8,128)(2,1)S(1)}, u32[]{:S(2)}, u32[]{:S(2)}) collective-permute-start(bf16[256,512]{1,0:T(8,128)(2,1)S(1)} %bitcast.172), channel_id=1, source_target_pairs={{0,2},{2,4},{4,6},{6,8},{8,10},{10,12},{12,14},{14,0},{1,3},{3,5},... | collective-permute-start | bytes 786440 | tf_op jit(solution)/shard_map/ppermute | solution.py:24
  15.0 3.1 %collective-permute-start.4 = (bf16[256,512]{1,0:T(8,128)(2,1)S(1)}, bf16[256,512]{1,0:T(8,128)(2,1)S(1)}, u32[]{:S(2)}, u32[]{:S(2)}) collective-permute-start(bf16[256,512]{1,0:T(8,128)(2,1)S(1)} %bitcast.173), channel_id=1, source_target_pairs={{2,0},{4,2},{6,4},{8,6},{10,8},{12,10},{14,12},{0,14},{3,1},{5,3},... | collective-permute-start | bytes 786440 | tf_op jit(solution)/shard_map/ppermute | solution.py:26
  18.1 1.1 copy.66
  19.2 3.9 %all_to_all.74 = bf16[128,2,512]{0,2,1:T(8,128)(2,1)S(1)} all-to-all(bf16[128,2,512]{0,2,1:T(8,128)(2,1)S(1)} %bitcast.178), channel_id=1, replica_groups=mesh['group'=2,'blk'=8,'ulysses'=2] {'ulysses'}, dimensions={1} | all-to-all | bytes 524288 | tf_op jit(solution)/shard_map/all_to_all | solution.py:98
  24.0 2.4 %copy.60 = bf16[128,8192]{0,1:T(8,128)(2,1)} copy(bf16[128,8192]{1,0:T(8,128)(2,1)S(1)} %copy-done.1) | data formatting | bytes 4194304 | tf_op args[0]
  26.5 5.0 %all-to-all-start = ((bf16[128,2,4096]{0,2,1:T(8,128)(2,1)}), bf16[128,2,4096]{0,2,1:T(8,128)(2,1)}, u32[]{:S(2)}, u32[]{:S(2)}) async-start(bf16[128,2,4096]{0,2,1:T(8,128)(2,1)} %bitcast.27), calls=%async_computation | async-start | bytes 4194304 | tf_op jit(solution)/shard_map/all_to_all | solution.py:96
  32.3 17.2 %collective-permute-done.1 = bf16[256,512]{1,0:T(8,128)(2,1)S(1)} collective-permute-done((bf16[256,512]{1,0:T(8,128)(2,1)S(1)}, bf16[256,512]{1,0:T(8,128)(2,1)S(1)}, u32[]{:S(2)}, u32[]{:S(2)}) %collective-permute-start.1) | collective-permute-done | bytes 262176 | tf_op jit(solution)/shard_map/ppermute | solution.py:24
  49.6 4.8 %collective-permute-start.5 = (bf16[256,512]{1,0:T(8,128)(2,1)S(1)}, bf16[256,512]{1,0:T(8,128)(2,1)S(1)}, u32[]{:S(2)}, u32[]{:S(2)}) collective-permute-start(bf16[256,512]{1,0:T(8,128)(2,1)S(1)} %collective-permute-done.4), channel_id=1, source_target_pairs={{2,0},{4,2},{6,4},{8,6},{10,8},{12,10},{14,12},{0,14},{3,1},{5,3},... | collective-permute-start | bytes 786440 | tf_op jit(solution)/shard_map/ppermute | solution.py:26
  54.4 11.8 %collective-permute-done.2 = bf16[256,512]{1,0:T(8,128)(2,1)S(1)} collective-permute-done((bf16[256,512]{1,0:T(8,128)(2,1)S(1)}, bf16[256,512]{1,0:T(8,128)(2,1)S(1)}, u32[]{:S(2)}, u32[]{:S(2)}) %collective-permute-start.2) | collective-permute-done | bytes 262176 | tf_op jit(solution)/shard_map/ppermute | solution.py:24
  66.1 2.5 %collective-permute-start.3 = (bf16[256,512]{1,0:T(8,128)(2,1)S(1)}, bf16[256,512]{1,0:T(8,128)(2,1)S(1)}, u32[]{:S(2)}, u32[]{:S(2)}) collective-permute-start(bf16[256,512]{1,0:T(8,128)(2,1)S(1)} %collective-permute-done.2), channel_id=1, source_target_pairs={{0,2},{2,4},{4,6},{6,8},{8,10},{10,12},{12,14},{14,0},{1,3},{3,5},... | collective-permute-start | bytes 786440 | tf_op jit(solution)/shard_map/ppermute | solution.py:24
  68.9 1.5 gather_fusion.3
  70.6 5.1 %collective-permute-start.6 = (bf16[256,512]{1,0:T(8,128)(2,1)S(1)}, bf16[256,512]{1,0:T(8,128)(2,1)S(1)}, u32[]{:S(2)}, u32[]{:S(2)}) collective-permute-start(bf16[256,512]{1,0:T(8,128)(2,1)S(1)} %collective-permute-done.5), channel_id=1, source_target_pairs={{2,0},{4,2},{6,4},{8,6},{10,8},{12,10},{14,12},{0,14},{3,1},{5,3},... | collective-permute-start | bytes 786440 | tf_op jit(solution)/shard_map/ppermute | solution.py:26
  75.7 7.3 %collective-permute-done.3 = bf16[256,512]{1,0:T(8,128)(2,1)S(1)} collective-permute-done((bf16[256,512]{1,0:T(8,128)(2,1)S(1)}, bf16[256,512]{1,0:T(8,128)(2,1)S(1)}, u32[]{:S(2)}, u32[]{:S(2)}) %collective-permute-start.3) | collective-permute-done | bytes 262176 | tf_op jit(solution)/shard_map/ppermute | solution.py:24
  88.8 2.3 %gather_fusion = bf16[8,256,512]{2,1,0:T(8,128)(2,1)S(1)} fusion(bf16[8,256,512]{2,1,0:T(8,128)(2,1)} %bitcast_dynamic-update-slice_fusion.1, s32[1024]{0:T(1024)S(1)} %pad_clamp_fusion), kind=kCustom, calls=%fused_computation | custom fusion | bytes 4194336 | tf_op jit(solution)/shard_map/gather | solution.py:29
  91.1 2.1 reshape.195
  93.2 2.1 copy.65
  95.4 3.1 %gather_fusion.1 = bf16[128,128,128]{2,1,0:T(8,128)(2,1)} fusion(bf16[16,128,4,128]{3,1,2,0:T(8,128)(2,1)S(1)} %copy.65, s32[128]{0:T(128)S(1)} %reshape.172), kind=kCustom, calls=%fused_computation.1 | custom fusion | bytes 8389632 | tf_op jit(solution)/shard_map/gather | solution.py:52
  98.5 4.0 %reshape.196 = bf16[16,128,4,128]{3,2,1,0:T(4,128)(2,1)} reshape(bf16[2048,512]{1,0:T(8,128)(2,1)} %all-gather.2.cloned.1.call-done) | data formatting | bytes 4194304 | tf_op jit(solution)/shard_map/reshape | solution.py:50
  102.5 2.1 copy.69
  104.7 3.1 %gather_fusion.2 = bf16[128,128,128]{2,1,0:T(8,128)(2,1)} fusion(bf16[16,128,4,128]{3,1,2,0:T(8,128)(2,1)S(1)} %copy.69, s32[128]{0:T(128)S(1)} %reshape.172), kind=kCustom, calls=%fused_computation.2 | custom fusion | bytes 8389632 | tf_op jit(solution)/shard_map/gather | solution.py:52
  107.8 89.8 %while.21 = (s32[]{:T(128)}, bf16[2,128,4,8,128]{1,4,3,2,0:T(8,128)(2,1)}, bf16[2,128,4,8,128]{1,4,3,2,0:T(8,128)(2,1)}, f32[2,4,8]{2,1,0:T(4,128)S(1)}, bf16[2,...) while((s32[]{:T(128)}, ...), condition=%wide.region_6.7_spmd, body=%wide.region_1.6_spmd.sunk | while | flops 1108097024 | bytes 46721236 | solution.py:125
  107.8 1.7 constant_dynamic-slice_fusion.13
  109.5 2.6 %copy.88 = bf16[1,4,16,128,128]{3,4,2,1,0:T(8,128)(2,1)} copy(bf16[1,4,16,128,128]{4,3,2,1,0:T(8,128)(2,1)S(1)} %constant_dynamic-slice_fusion.13) | data formatting | bytes 4194304 | tf_op jit(solution)/shard_map/while/body/jit(dynamic_index_in_dim)/dynamic_slice | solution.py:125
  112.1 1.3 constant_dynamic-slice_fusion.14
  113.4 1.3 copy.89
  114.8 1.7 dynamic-slice_bitcast_fusion.6
  116.5 35.1 %while.22 = (s32[]{:T(128)}, bf16[4,128,8,128]{1,3,2,0:T(8,128)(2,1)S(1)}, bf16[4,16,128,128]{2,3,1,0:T(8,128)(2,1)}, pred[4,16]{1,0:T(4,128)(4,1)S(1)}, pred[4,...) while((s32[]{:T(128)}, ...), condition=%wide.region_5.5_spmd, body=%wide.region_2.4_spmd.sunk | while | flops 1108097024 | bytes 27845104 | solution.py:79
  116.9 2.4 %fusion.60 = (f32[8,128]{1,0:T(8,128)S(1)}, f32[16,128,128,8]{2,1,3,0:T(8,128)S(1)}) fusion(f32[16]{0:T(128)S(1)} %fusion.57, f32[8]{0:T(128)S(1)} %fusion.58, pred[128,16,128]{0,2,1:T(8,128)(4,1)S(1)} %or_and_fusion.2, bf16[4,128,8,128]{3,1,2,0:T(8,128)(2,1)} %get-tuple-element.362, s32[]{:T(128)} %get-tuple-element.346, ...), kind=kOutput, calls=%fused_computation.8.clone.1 | convolution fusion | flops 545258496 | bytes 9443328 | tf_op jit(solution)/shard_map/while/body/eval_jaxpr/while/body/eval_jaxpr/tpd,nsd->ptns/dot_general | solution.py:57
  119.3 2.4 %fusion.61 = f32[8,128]{1,0:T(8,128)S(1)} fusion(f32[16,128,128,8]{2,1,3,0:T(8,128)S(1)} %get-tuple-element.334, f32[8,128]{1,0:T(8,128)S(1)} %get-tuple-element.335, f32[16]{0:T(128)S(1)} %fusion.57, f32[8]{0:T(128)S(1)} %fusion.58, pred[128,16,128]{0,2,1:T(8,128)(4,1)S(1)} %or_and_fusion.2), kind=kLoop, calls=%fused_computation.6.clone.1 | loop fusion | flops 12581888 | bytes 8659040 | tf_op jit(solution)/shard_map/while/body/eval_jaxpr/while/body/eval_jaxpr/reduce_sum | solution.py:67
  121.7 3.6 %fusion.62 = bf16[4,128,8,128]{1,3,2,0:T(8,128)(2,1)S(1)} fusion(bf16[4,128,8,128]{1,3,2,0:T(8,128)(2,1)S(1)} %get-tuple-element.347, s32[]{:T(128)} %get-tuple-element.346, f32[16,128,128,8]{2,1,3,0:T(8,128)S(1)} %get-tuple-element.334, f32[8,128]{1,0:T(8,128)S(1)} %get-tuple-element.335, f32[16]{0:T(128)S(1)} %fusion.57, f32[8]{0:T(128)S(1)} %fusion.58, ...), kind=kOutput, calls=%fused_computation.15.clone.1 | convolution fusion | flops 549715968 | bytes 9447424 | tf_op jit(solution)/shard_map/while/body/eval_jaxpr/while/body/eval_jaxpr/ptns,nsd->tpd/dot_general | solution.py:68
  125.6 2.4 %fusion.60 = (f32[8,128]{1,0:T(8,128)S(1)}, f32[16,128,128,8]{2,1,3,0:T(8,128)S(1)}) fusion(f32[16]{0:T(128)S(1)} %fusion.57, f32[8]{0:T(128)S(1)} %fusion.58, pred[128,16,128]{0,2,1:T(8,128)(4,1)S(1)} %or_and_fusion.2, bf16[4,128,8,128]{3,1,2,0:T(8,128)(2,1)} %get-tuple-element.362, s32[]{:T(128)} %get-tuple-element.346, ...), kind=kOutput, calls=%fused_computation.8.clone.1 | convolution fusion | flops 545258496 | bytes 9443328 | tf_op jit(solution)/shard_map/while/body/eval_jaxpr/while/body/eval_jaxpr/tpd,nsd->ptns/dot_general | solution.py:57
  128.0 2.4 %fusion.61 = f32[8,128]{1,0:T(8,128)S(1)} fusion(f32[16,128,128,8]{2,1,3,0:T(8,128)S(1)} %get-tuple-element.334, f32[8,128]{1,0:T(8,128)S(1)} %get-tuple-element.335, f32[16]{0:T(128)S(1)} %fusion.57, f32[8]{0:T(128)S(1)} %fusion.58, pred[128,16,128]{0,2,1:T(8,128)(4,1)S(1)} %or_and_fusion.2), kind=kLoop, calls=%fused_computation.6.clone.1 | loop fusion | flops 12581888 | bytes 8659040 | tf_op jit(solution)/shard_map/while/body/eval_jaxpr/while/body/eval_jaxpr/reduce_sum | solution.py:67
  130.5 3.6 %fusion.62 = bf16[4,128,8,128]{1,3,2,0:T(8,128)(2,1)S(1)} fusion(bf16[4,128,8,128]{1,3,2,0:T(8,128)(2,1)S(1)} %get-tuple-element.347, s32[]{:T(128)} %get-tuple-element.346, f32[16,128,128,8]{2,1,3,0:T(8,128)S(1)} %get-tuple-element.334, f32[8,128]{1,0:T(8,128)S(1)} %get-tuple-element.335, f32[16]{0:T(128)S(1)} %fusion.57, f32[8]{0:T(128)S(1)} %fusion.58, ...), kind=kOutput, calls=%fused_computation.15.clone.1 | convolution fusion | flops 549715968 | bytes 9447424 | tf_op jit(solution)/shard_map/while/body/eval_jaxpr/while/body/eval_jaxpr/ptns,nsd->tpd/dot_general | solution.py:68
  134.4 2.4 %fusion.60 = (f32[8,128]{1,0:T(8,128)S(1)}, f32[16,128,128,8]{2,1,3,0:T(8,128)S(1)}) fusion(f32[16]{0:T(128)S(1)} %fusion.57, f32[8]{0:T(128)S(1)} %fusion.58, pred[128,16,128]{0,2,1:T(8,128)(4,1)S(1)} %or_and_fusion.2, bf16[4,128,8,128]{3,1,2,0:T(8,128)(2,1)} %get-tuple-element.362, s32[]{:T(128)} %get-tuple-element.346, ...), kind=kOutput, calls=%fused_computation.8.clone.1 | convolution fusion | flops 545258496 | bytes 9443328 | tf_op jit(solution)/shard_map/while/body/eval_jaxpr/while/body/eval_jaxpr/tpd,nsd->ptns/dot_general | solution.py:57
  136.8 2.4 %fusion.61 = f32[8,128]{1,0:T(8,128)S(1)} fusion(f32[16,128,128,8]{2,1,3,0:T(8,128)S(1)} %get-tuple-element.334, f32[8,128]{1,0:T(8,128)S(1)} %get-tuple-element.335, f32[16]{0:T(128)S(1)} %fusion.57, f32[8]{0:T(128)S(1)} %fusion.58, pred[128,16,128]{0,2,1:T(8,128)(4,1)S(1)} %or_and_fusion.2), kind=kLoop, calls=%fused_computation.6.clone.1 | loop fusion | flops 12581888 | bytes 8659040 | tf_op jit(solution)/shard_map/while/body/eval_jaxpr/while/body/eval_jaxpr/reduce_sum | solution.py:67
  139.2 3.6 %fusion.62 = bf16[4,128,8,128]{1,3,2,0:T(8,128)(2,1)S(1)} fusion(bf16[4,128,8,128]{1,3,2,0:T(8,128)(2,1)S(1)} %get-tuple-element.347, s32[]{:T(128)} %get-tuple-element.346, f32[16,128,128,8]{2,1,3,0:T(8,128)S(1)} %get-tuple-element.334, f32[8,128]{1,0:T(8,128)S(1)} %get-tuple-element.335, f32[16]{0:T(128)S(1)} %fusion.57, f32[8]{0:T(128)S(1)} %fusion.58, ...), kind=kOutput, calls=%fused_computation.15.clone.1 | convolution fusion | flops 549715968 | bytes 9447424 | tf_op jit(solution)/shard_map/while/body/eval_jaxpr/while/body/eval_jaxpr/ptns,nsd->tpd/dot_general | solution.py:68
  143.2 2.4 %fusion.60 = (f32[8,128]{1,0:T(8,128)S(1)}, f32[16,128,128,8]{2,1,3,0:T(8,128)S(1)}) fusion(f32[16]{0:T(128)S(1)} %fusion.57, f32[8]{0:T(128)S(1)} %fusion.58, pred[128,16,128]{0,2,1:T(8,128)(4,1)S(1)} %or_and_fusion.2, bf16[4,128,8,128]{3,1,2,0:T(8,128)(2,1)} %get-tuple-element.362, s32[]{:T(128)} %get-tuple-element.346, ...), kind=kOutput, calls=%fused_computation.8.clone.1 | convolution fusion | flops 545258496 | bytes 9443328 | tf_op jit(solution)/shard_map/while/body/eval_jaxpr/while/body/eval_jaxpr/tpd,nsd->ptns/dot_general | solution.py:57
  145.6 2.4 %fusion.61 = f32[8,128]{1,0:T(8,128)S(1)} fusion(f32[16,128,128,8]{2,1,3,0:T(8,128)S(1)} %get-tuple-element.334, f32[8,128]{1,0:T(8,128)S(1)} %get-tuple-element.335, f32[16]{0:T(128)S(1)} %fusion.57, f32[8]{0:T(128)S(1)} %fusion.58, pred[128,16,128]{0,2,1:T(8,128)(4,1)S(1)} %or_and_fusion.2), kind=kLoop, calls=%fused_computation.6.clone.1 | loop fusion | flops 12581888 | bytes 8659040 | tf_op jit(solution)/shard_map/while/body/eval_jaxpr/while/body/eval_jaxpr/reduce_sum | solution.py:67
  148.0 3.6 %fusion.62 = bf16[4,128,8,128]{1,3,2,0:T(8,128)(2,1)S(1)} fusion(bf16[4,128,8,128]{1,3,2,0:T(8,128)(2,1)S(1)} %get-tuple-element.347, s32[]{:T(128)} %get-tuple-element.346, f32[16,128,128,8]{2,1,3,0:T(8,128)S(1)} %get-tuple-element.334, f32[8,128]{1,0:T(8,128)S(1)} %get-tuple-element.335, f32[16]{0:T(128)S(1)} %fusion.57, f32[8]{0:T(128)S(1)} %fusion.58, ...), kind=kOutput, calls=%fused_computation.15.clone.1 | convolution fusion | flops 549715968 | bytes 9447424 | tf_op jit(solution)/shard_map/while/body/eval_jaxpr/while/body/eval_jaxpr/ptns,nsd->tpd/dot_general | solution.py:68
  151.6 1.0 bitcast_dynamic-update-slice_fusion.10
  152.7 1.7 constant_dynamic-slice_fusion.13
  154.4 2.6 %copy.88 = bf16[1,4,16,128,128]{3,4,2,1,0:T(8,128)(2,1)} copy(bf16[1,4,16,128,128]{4,3,2,1,0:T(8,128)(2,1)S(1)} %constant_dynamic-slice_fusion.13) | data formatting | bytes 4194304 | tf_op jit(solution)/shard_map/while/body/jit(dynamic_index_in_dim)/dynamic_slice | solution.py:125
  157.0 1.3 constant_dynamic-slice_fusion.14
  158.3 1.3 copy.89
  159.7 1.7 dynamic-slice_bitcast_fusion.6
  161.4 35.1 %while.22 = (s32[]{:T(128)}, bf16[4,128,8,128]{1,3,2,0:T(8,128)(2,1)S(1)}, bf16[4,16,128,128]{2,3,1,0:T(8,128)(2,1)}, pred[4,16]{1,0:T(4,128)(4,1)S(1)}, pred[4,...) while((s32[]{:T(128)}, ...), condition=%wide.region_5.5_spmd, body=%wide.region_2.4_spmd.sunk | while | flops 1108097024 | bytes 27845104 | solution.py:79
  161.8 2.4 %fusion.60 = (f32[8,128]{1,0:T(8,128)S(1)}, f32[16,128,128,8]{2,1,3,0:T(8,128)S(1)}) fusion(f32[16]{0:T(128)S(1)} %fusion.57, f32[8]{0:T(128)S(1)} %fusion.58, pred[128,16,128]{0,2,1:T(8,128)(4,1)S(1)} %or_and_fusion.2, bf16[4,128,8,128]{3,1,2,0:T(8,128)(2,1)} %get-tuple-element.362, s32[]{:T(128)} %get-tuple-element.346, ...), kind=kOutput, calls=%fused_computation.8.clone.1 | convolution fusion | flops 545258496 | bytes 9443328 | tf_op jit(solution)/shard_map/while/body/eval_jaxpr/while/body/eval_jaxpr/tpd,nsd->ptns/dot_general | solution.py:57
  164.2 2.4 %fusion.61 = f32[8,128]{1,0:T(8,128)S(1)} fusion(f32[16,128,128,8]{2,1,3,0:T(8,128)S(1)} %get-tuple-element.334, f32[8,128]{1,0:T(8,128)S(1)} %get-tuple-element.335, f32[16]{0:T(128)S(1)} %fusion.57, f32[8]{0:T(128)S(1)} %fusion.58, pred[128,16,128]{0,2,1:T(8,128)(4,1)S(1)} %or_and_fusion.2), kind=kLoop, calls=%fused_computation.6.clone.1 | loop fusion | flops 12581888 | bytes 8659040 | tf_op jit(solution)/shard_map/while/body/eval_jaxpr/while/body/eval_jaxpr/reduce_sum | solution.py:67
  166.6 3.6 %fusion.62 = bf16[4,128,8,128]{1,3,2,0:T(8,128)(2,1)S(1)} fusion(bf16[4,128,8,128]{1,3,2,0:T(8,128)(2,1)S(1)} %get-tuple-element.347, s32[]{:T(128)} %get-tuple-element.346, f32[16,128,128,8]{2,1,3,0:T(8,128)S(1)} %get-tuple-element.334, f32[8,128]{1,0:T(8,128)S(1)} %get-tuple-element.335, f32[16]{0:T(128)S(1)} %fusion.57, f32[8]{0:T(128)S(1)} %fusion.58, ...), kind=kOutput, calls=%fused_computation.15.clone.1 | convolution fusion | flops 549715968 | bytes 9447424 | tf_op jit(solution)/shard_map/while/body/eval_jaxpr/while/body/eval_jaxpr/ptns,nsd->tpd/dot_general | solution.py:68
  170.5 2.4 %fusion.60 = (f32[8,128]{1,0:T(8,128)S(1)}, f32[16,128,128,8]{2,1,3,0:T(8,128)S(1)}) fusion(f32[16]{0:T(128)S(1)} %fusion.57, f32[8]{0:T(128)S(1)} %fusion.58, pred[128,16,128]{0,2,1:T(8,128)(4,1)S(1)} %or_and_fusion.2, bf16[4,128,8,128]{3,1,2,0:T(8,128)(2,1)} %get-tuple-element.362, s32[]{:T(128)} %get-tuple-element.346, ...), kind=kOutput, calls=%fused_computation.8.clone.1 | convolution fusion | flops 545258496 | bytes 9443328 | tf_op jit(solution)/shard_map/while/body/eval_jaxpr/while/body/eval_jaxpr/tpd,nsd->ptns/dot_general | solution.py:57
  173.0 2.4 %fusion.61 = f32[8,128]{1,0:T(8,128)S(1)} fusion(f32[16,128,128,8]{2,1,3,0:T(8,128)S(1)} %get-tuple-element.334, f32[8,128]{1,0:T(8,128)S(1)} %get-tuple-element.335, f32[16]{0:T(128)S(1)} %fusion.57, f32[8]{0:T(128)S(1)} %fusion.58, pred[128,16,128]{0,2,1:T(8,128)(4,1)S(1)} %or_and_fusion.2), kind=kLoop, calls=%fused_computation.6.clone.1 | loop fusion | flops 12581888 | bytes 8659040 | tf_op jit(solution)/shard_map/while/body/eval_jaxpr/while/body/eval_jaxpr/reduce_sum | solution.py:67
  175.4 3.6 %fusion.62 = bf16[4,128,8,128]{1,3,2,0:T(8,128)(2,1)S(1)} fusion(bf16[4,128,8,128]{1,3,2,0:T(8,128)(2,1)S(1)} %get-tuple-element.347, s32[]{:T(128)} %get-tuple-element.346, f32[16,128,128,8]{2,1,3,0:T(8,128)S(1)} %get-tuple-element.334, f32[8,128]{1,0:T(8,128)S(1)} %get-tuple-element.335, f32[16]{0:T(128)S(1)} %fusion.57, f32[8]{0:T(128)S(1)} %fusion.58, ...), kind=kOutput, calls=%fused_computation.15.clone.1 | convolution fusion | flops 549715968 | bytes 9447424 | tf_op jit(solution)/shard_map/while/body/eval_jaxpr/while/body/eval_jaxpr/ptns,nsd->tpd/dot_general | solution.py:68
  179.3 2.4 %fusion.60 = (f32[8,128]{1,0:T(8,128)S(1)}, f32[16,128,128,8]{2,1,3,0:T(8,128)S(1)}) fusion(f32[16]{0:T(128)S(1)} %fusion.57, f32[8]{0:T(128)S(1)} %fusion.58, pred[128,16,128]{0,2,1:T(8,128)(4,1)S(1)} %or_and_fusion.2, bf16[4,128,8,128]{3,1,2,0:T(8,128)(2,1)} %get-tuple-element.362, s32[]{:T(128)} %get-tuple-element.346, ...), kind=kOutput, calls=%fused_computation.8.clone.1 | convolution fusion | flops 545258496 | bytes 9443328 | tf_op jit(solution)/shard_map/while/body/eval_jaxpr/while/body/eval_jaxpr/tpd,nsd->ptns/dot_general | solution.py:57
  181.7 2.4 %fusion.61 = f32[8,128]{1,0:T(8,128)S(1)} fusion(f32[16,128,128,8]{2,1,3,0:T(8,128)S(1)} %get-tuple-element.334, f32[8,128]{1,0:T(8,128)S(1)} %get-tuple-element.335, f32[16]{0:T(128)S(1)} %fusion.57, f32[8]{0:T(128)S(1)} %fusion.58, pred[128,16,128]{0,2,1:T(8,128)(4,1)S(1)} %or_and_fusion.2), kind=kLoop, calls=%fused_computation.6.clone.1 | loop fusion | flops 12581888 | bytes 8659040 | tf_op jit(solution)/shard_map/while/body/eval_jaxpr/while/body/eval_jaxpr/reduce_sum | solution.py:67
  184.2 3.6 %fusion.62 = bf16[4,128,8,128]{1,3,2,0:T(8,128)(2,1)S(1)} fusion(bf16[4,128,8,128]{1,3,2,0:T(8,128)(2,1)S(1)} %get-tuple-element.347, s32[]{:T(128)} %get-tuple-element.346, f32[16,128,128,8]{2,1,3,0:T(8,128)S(1)} %get-tuple-element.334, f32[8,128]{1,0:T(8,128)S(1)} %get-tuple-element.335, f32[16]{0:T(128)S(1)} %fusion.57, f32[8]{0:T(128)S(1)} %fusion.58, ...), kind=kOutput, calls=%fused_computation.15.clone.1 | convolution fusion | flops 549715968 | bytes 9447424 | tf_op jit(solution)/shard_map/while/body/eval_jaxpr/while/body/eval_jaxpr/ptns,nsd->tpd/dot_general | solution.py:68
  188.1 2.4 %fusion.60 = (f32[8,128]{1,0:T(8,128)S(1)}, f32[16,128,128,8]{2,1,3,0:T(8,128)S(1)}) fusion(f32[16]{0:T(128)S(1)} %fusion.57, f32[8]{0:T(128)S(1)} %fusion.58, pred[128,16,128]{0,2,1:T(8,128)(4,1)S(1)} %or_and_fusion.2, bf16[4,128,8,128]{3,1,2,0:T(8,128)(2,1)} %get-tuple-element.362, s32[]{:T(128)} %get-tuple-element.346, ...), kind=kOutput, calls=%fused_computation.8.clone.1 | convolution fusion | flops 545258496 | bytes 9443328 | tf_op jit(solution)/shard_map/while/body/eval_jaxpr/while/body/eval_jaxpr/tpd,nsd->ptns/dot_general | solution.py:57
  190.5 2.4 %fusion.61 = f32[8,128]{1,0:T(8,128)S(1)} fusion(f32[16,128,128,8]{2,1,3,0:T(8,128)S(1)} %get-tuple-element.334, f32[8,128]{1,0:T(8,128)S(1)} %get-tuple-element.335, f32[16]{0:T(128)S(1)} %fusion.57, f32[8]{0:T(128)S(1)} %fusion.58, pred[128,16,128]{0,2,1:T(8,128)(4,1)S(1)} %or_and_fusion.2), kind=kLoop, calls=%fused_computation.6.clone.1 | loop fusion | flops 12581888 | bytes 8659040 | tf_op jit(solution)/shard_map/while/body/eval_jaxpr/while/body/eval_jaxpr/reduce_sum | solution.py:67
  192.9 3.6 %fusion.62 = bf16[4,128,8,128]{1,3,2,0:T(8,128)(2,1)S(1)} fusion(bf16[4,128,8,128]{1,3,2,0:T(8,128)(2,1)S(1)} %get-tuple-element.347, s32[]{:T(128)} %get-tuple-element.346, f32[16,128,128,8]{2,1,3,0:T(8,128)S(1)} %get-tuple-element.334, f32[8,128]{1,0:T(8,128)S(1)} %get-tuple-element.335, f32[16]{0:T(128)S(1)} %fusion.57, f32[8]{0:T(128)S(1)} %fusion.58, ...), kind=kOutput, calls=%fused_computation.15.clone.1 | convolution fusion | flops 549715968 | bytes 9447424 | tf_op jit(solution)/shard_map/while/body/eval_jaxpr/while/body/eval_jaxpr/ptns,nsd->tpd/dot_general | solution.py:68
  197.6 2.9 %copy.83 = bf16[2,128,4096]{2,1,0:T(8,128)(2,1)S(1)} copy(bf16[2,128,4096]{1,2,0:T(8,128)(2,1)} %bitcast.170) | data formatting | bytes 4194304 | tf_op jit(solution)/shard_map/all_to_all | solution.py:130
  200.5 6.3 %all_to_all.75 = bf16[2,128,4096]{2,1,0:T(8,128)(2,1)} all-to-all(bf16[2,128,4096]{2,1,0:T(8,128)(2,1)S(1)} %copy.83), channel_id=1, replica_groups=mesh['group'=2,'blk'=8,'ulysses'=2] {'ulysses'}, dimensions={0} | all-to-all | bytes 4194304 | tf_op jit(solution)/shard_map/all_to_all | solution.py:130
  206.8 3.1 %copy.73 = bf16[2,128,4096]{1,2,0:T(8,128)(2,1)S(1)} copy(bf16[2,128,4096]{2,1,0:T(8,128)(2,1)} %all_to_all.75) | data formatting | bytes 4194304 | tf_op jit(solution)/shard_map/all_to_all | solution.py:130
  210.0 2.9 %copy.74 = bf16[128,8192]{1,0:T(8,128)(2,1)} copy(bf16[128,8192]{0,1:T(8,128)(2,1)S(1)} %bitcast.168) | data formatting | bytes 4194304 | tf_op jit(solution)/shard_map/all_to_all | solution.py:130
  (99 shorter events, 11.5 us)
Async XLA Ops:
  6.5 62.3 %copy-start = (bf16[16,8]{0,1:T(8,128)(2,1)S(1)}, bf16[16,8]{0,1:T(8,128)(2,1)}, u32[]{:S(2)}) copy-start(bf16[16,8]{0,1:T(8,128)(2,1)} %param.15) | copy-start | bytes 772
  6.5 17.5 %copy-start.1 = (bf16[128,8192]{1,0:T(8,128)(2,1)S(1)}, bf16[128,8192]{1,0:T(8,128)(2,1)}, u32[]{:S(2)}) copy-start(bf16[128,8192]{1,0:T(8,128)(2,1)} %param.11) | copy-start | bytes 6291460
  6.5 91.9 %all-gather.2.cloned.1.call-start = ((), (), s32[]{:S(2)}) async-start(), calls=%async_computation.4 | async-start | bytes 2359296 | tf_op jit(solution)/shard_map/all_gather | solution.py:119
  11.9 20.2 %collective-permute-start = (bf16[256,512]{1,0:T(8,128)(2,1)S(1)}, bf16[256,512]{1,0:T(8,128)(2,1)S(1)}, u32[]{:S(2)}, u32[]{:S(2)}) collective-permute-start(bf16[256,512]{1,0:T(8,128)(2,1)S(1)} %bitcast.172), channel_id=1, source_target_pairs={{0,2},{2,4},{4,6},{6,8},{8,10},{10,12},{12,14},{14,0},{1,3},{3,5},... | collective-permute-start | bytes 786440 | tf_op jit(solution)/shard_map/ppermute | solution.py:24
  15.0 34.6 %collective-permute-start.4 = (bf16[256,512]{1,0:T(8,128)(2,1)S(1)}, bf16[256,512]{1,0:T(8,128)(2,1)S(1)}, u32[]{:S(2)}, u32[]{:S(2)}) collective-permute-start(bf16[256,512]{1,0:T(8,128)(2,1)S(1)} %bitcast.173), channel_id=1, source_target_pairs={{2,0},{4,2},{6,4},{8,6},{10,8},{12,10},{14,12},{0,14},{3,1},{5,3},... | collective-permute-start | bytes 786440 | tf_op jit(solution)/shard_map/ppermute | solution.py:26
  26.5 5.1 %copy-start.2 = (s32[8,8]{1,0:T(8,128)S(1)}, s32[8,8]{1,0:T(8,128)}, u32[]{:S(2)}) copy-start(s32[8,8]{1,0:T(8,128)} %param.17) | copy-start | bytes 772
  26.5 5.1 %copy-start.3 = (s32[8,8]{1,0:T(8,128)S(1)}, s32[8,8]{1,0:T(8,128)}, u32[]{:S(2)}) copy-start(s32[8,8]{1,0:T(8,128)} %param.16) | copy-start | bytes 772
  26.5 42.1 %copy-start.4 = (bf16[2,64]{1,0:T(2,128)(2,1)S(1)}, bf16[2,64]{1,0:T(2,128)(2,1)}, u32[]{:S(2)}) copy-start(bf16[2,64]{1,0:T(2,128)(2,1)} %param.14) | copy-start | bytes 772
  26.5 81.3 %all-to-all-start = ((bf16[128,2,4096]{0,2,1:T(8,128)(2,1)}), bf16[128,2,4096]{0,2,1:T(8,128)(2,1)}, u32[]{:S(2)}, u32[]{:S(2)}) async-start(bf16[128,2,4096]{0,2,1:T(8,128)(2,1)} %bitcast.27), calls=%async_computation | async-start | bytes 4194304 | tf_op jit(solution)/shard_map/all_to_all | solution.py:96
  32.1 17.4 %collective-permute-start.1 = (bf16[256,512]{1,0:T(8,128)(2,1)S(1)}, bf16[256,512]{1,0:T(8,128)(2,1)S(1)}, u32[]{:S(2)}, u32[]{:S(2)}) collective-permute-start(bf16[256,512]{1,0:T(8,128)(2,1)S(1)} %collective-permute-done), channel_id=1, source_target_pairs={{0,2},{2,4},{4,6},{6,8},{8,10},{10,12},{12,14},{14,0},{1,3},{3,5},... | collective-permute-start | bytes 786440 | tf_op jit(solution)/shard_map/ppermute | solution.py:24
  49.5 16.7 %collective-permute-start.2 = (bf16[256,512]{1,0:T(8,128)(2,1)S(1)}, bf16[256,512]{1,0:T(8,128)(2,1)S(1)}, u32[]{:S(2)}, u32[]{:S(2)}) collective-permute-start(bf16[256,512]{1,0:T(8,128)(2,1)S(1)} %collective-permute-done.1), channel_id=1, source_target_pairs={{0,2},{2,4},{4,6},{6,8},{8,10},{10,12},{12,14},{14,0},{1,3},{3,5},... | collective-permute-start | bytes 786440 | tf_op jit(solution)/shard_map/ppermute | solution.py:24
  49.6 21.0 %collective-permute-start.5 = (bf16[256,512]{1,0:T(8,128)(2,1)S(1)}, bf16[256,512]{1,0:T(8,128)(2,1)S(1)}, u32[]{:S(2)}, u32[]{:S(2)}) collective-permute-start(bf16[256,512]{1,0:T(8,128)(2,1)S(1)} %collective-permute-done.4), channel_id=1, source_target_pairs={{2,0},{4,2},{6,4},{8,6},{10,8},{12,10},{14,12},{0,14},{3,1},{5,3},... | collective-permute-start | bytes 786440 | tf_op jit(solution)/shard_map/ppermute | solution.py:26
  66.1 16.9 %collective-permute-start.3 = (bf16[256,512]{1,0:T(8,128)(2,1)S(1)}, bf16[256,512]{1,0:T(8,128)(2,1)S(1)}, u32[]{:S(2)}, u32[]{:S(2)}) collective-permute-start(bf16[256,512]{1,0:T(8,128)(2,1)S(1)} %collective-permute-done.2), channel_id=1, source_target_pairs={{0,2},{2,4},{4,6},{6,8},{8,10},{10,12},{12,14},{14,0},{1,3},{3,5},... | collective-permute-start | bytes 786440 | tf_op jit(solution)/shard_map/ppermute | solution.py:24
  70.6 17.5 %collective-permute-start.6 = (bf16[256,512]{1,0:T(8,128)(2,1)S(1)}, bf16[256,512]{1,0:T(8,128)(2,1)S(1)}, u32[]{:S(2)}, u32[]{:S(2)}) collective-permute-start(bf16[256,512]{1,0:T(8,128)(2,1)S(1)} %collective-permute-done.5), channel_id=1, source_target_pairs={{2,0},{4,2},{6,4},{8,6},{10,8},{12,10},{14,12},{0,14},{3,1},{5,3},... | collective-permute-start | bytes 786440 | tf_op jit(solution)/shard_map/ppermute | solution.py:26
Sparse Core Ops, SparseCore 0:
  24.2 66.1 all-gather.1
